TPU v7x, 32 devices: a whole 2x2x4 slice. The times are simulated.
32 devices in a mesh: scene: 4 (over x, core), seq: 8 (over z, y).
Axes of the slice: x: 2, y: 2, z: 4, core: 2. Of those that a mesh axis runs over, the one named last changes fastest.
Arguments:
- tokens: bfloat16 [10240, 768], P(('scene', 'seq')), may hold values from -6 to 6
- scene_tokens: int32 [4], P('scene'), may hold values from 128 to 320, as said below
- cotangent: bfloat16 [10240, 768], P(('scene', 'seq')), may hold values from -6 to 6
- qkv_master: float32 [768, 2304], P(('scene', 'seq')), may hold values from -0.21875 to 0.21875
- out_master: float32 [768, 768], P(('scene', 'seq')), may hold values from -6 to 6
- up_master: float32 [768, 3072], P(('scene', 'seq')), may hold values from -0.21875 to 0.21875
- down_master: float32 [3072, 768], P(('scene', 'seq')), may hold values from -0.109375 to 0.109375
- gain_one: float32 [768], replicated, may hold values from 0.5 to 1.5
- gain_two: float32 [768], replicated, may hold values from 0.5 to 1.5
Outputs:
- mixed: bfloat16 [10240, 768], P(('scene', 'seq'))
- input_grad: float32 [10240, 768], P(('scene', 'seq'))
- qkv_grad: float32 [768, 2304], P(('scene', 'seq'))
- out_grad: float32 [768, 768], P(('scene', 'seq'))
- up_grad: float32 [768, 3072], P(('scene', 'seq'))
- down_grad: float32 [3072, 768], P(('scene', 'seq'))
- gain_one_grad: float32 [768], P(('scene', 'seq'))
- gain_two_grad: float32 [768], P(('scene', 'seq'))
Inputs may be any that keep to these rules, and one draw needn't show every extreme that they name: Slots 0 to scene_tokens[s] - 1 of every device of scene s's group hold that scene's tokens, the others are padding; one scene, drawn from the seed, has all 320 slots of every device live.
All inputs are finite; a program needn't handle non-finite values.
Results may differ from a plain program's by a relative error of at most 0.02.
Values may be sent and summed in bfloat16 or wider, within the bound.
No kernel may reach another device: no remote copies, remote signals or barrier semaphores. Data moves between devices by JAX's collectives and lax.ppermute only.
A program may use at most 512 MiB of HBM per device.

v0:
```python
import jax
import jax.numpy as jnp
from jax import lax
from jax.sharding import PartitionSpec as P

HEADS = 12
HEAD = 64
NEG_BIG = -1e30


def norm_rows(values, gain_vector):
    mean_value = jnp.mean(values, axis=-1, keepdims=True)
    centered = values - mean_value
    variance = jnp.mean(centered * centered, axis=-1, keepdims=True)
    inverse = lax.rsqrt(variance + 1e-05)
    scaled = centered * inverse
    return (scaled * gain_vector, scaled, inverse)


def norm_back(grad_result, scaled, inverse, gain_vector):
    grad_scaled = grad_result * gain_vector
    first_mean = jnp.mean(grad_scaled, axis=-1, keepdims=True)
    second_mean = jnp.mean(grad_scaled * scaled, axis=-1, keepdims=True)
    grad_input = inverse * (grad_scaled - first_mean - scaled * second_mean)
    return (grad_input, jnp.sum(grad_result * scaled, axis=0))


def split_heads(values):
    return values.reshape(values.shape[0], HEADS, HEAD)


def score_grads(query_part, grad_part, key_part, value_part, lse_part, delta_part, live_keys):
    scores = (
        jnp.einsum("qhd,khd->hqk", query_part, key_part, preferred_element_type=jnp.float32) * 0.125
    )
    weights_now = jnp.where(live_keys[None, None, :], jnp.exp(scores - lse_part[:, :, None]), 0.0)
    grad_weights = jnp.einsum(
        "qhd,khd->hqk", grad_part, value_part, preferred_element_type=jnp.float32
    )
    dscore = (weights_now * (grad_weights - delta_part[:, :, None])).astype(jnp.bfloat16)
    return (weights_now.astype(jnp.bfloat16), dscore)


def on_device(
    tokens,
    scene_tokens,
    cotangent,
    qkv_master,
    out_master,
    up_master,
    down_master,
    gain_one,
    gain_two,
):
    local_rows = tokens.shape[0]
    model_width = tokens.shape[1]
    live_count = scene_tokens[0]
    local_live = jnp.arange(local_rows, dtype=jnp.int32) < live_count
    qkv_part = qkv_master.astype(jnp.bfloat16)
    out_part = out_master.astype(jnp.bfloat16)
    up_part = up_master.astype(jnp.bfloat16)
    down_part = down_master.astype(jnp.bfloat16)
    qkv_weight, out_weight, up_weight, down_weight = (
        lax.all_gather(qkv_part, ("scene", "seq"), axis=0, tiled=True),
        lax.all_gather(out_part, ("scene", "seq"), axis=0, tiled=True),
        lax.all_gather(up_part, ("scene", "seq"), axis=0, tiled=True),
        lax.all_gather(down_part, ("scene", "seq"), axis=0, tiled=True),
    )
    inputs = tokens.astype(jnp.float32)
    normed_one, scaled_one, inverse_one = norm_rows(inputs, gain_one)
    normed_low = normed_one.astype(jnp.bfloat16)
    qkv_rows = jnp.dot(normed_low, qkv_weight, preferred_element_type=jnp.float32).astype(
        jnp.bfloat16
    )
    queries = qkv_rows[:, :model_width]
    key_rows = qkv_rows[:, model_width : 2 * model_width]
    value_rows = qkv_rows[:, 2 * model_width :]
    query_heads = split_heads(queries)

    def piece_live(piece_rows):
        places = jnp.arange(piece_rows, dtype=jnp.int32)
        return places % local_rows < live_count

    row_max = jnp.full((HEADS, local_rows), NEG_BIG, jnp.float32)
    key_piece = lax.all_gather(key_rows, "seq", axis=0, tiled=True)
    value_piece = lax.all_gather(value_rows, "seq", axis=0, tiled=True)
    piece_rows = key_piece.shape[0]
    scores = (
        jnp.einsum(
            "qhd,khd->hqk", query_heads, split_heads(key_piece), preferred_element_type=jnp.float32
        )
        * 0.125
    )
    scores = jnp.where(piece_live(piece_rows)[None, None, :], scores, NEG_BIG)
    new_max = jnp.maximum(row_max, jnp.max(scores, axis=-1))
    exponent = jnp.exp(scores - new_max[:, :, None])
    new_sum = jnp.sum(exponent, axis=-1)
    update = jnp.einsum(
        "hqk,khd->hqd",
        exponent.astype(jnp.bfloat16),
        split_heads(value_piece),
        preferred_element_type=jnp.float32,
    )
    row_lse = new_max + jnp.log(new_sum)
    attended = (
        (update / new_sum[:, :, None])
        .transpose(1, 0, 2)
        .reshape(local_rows, model_width)
        .astype(jnp.bfloat16)
    )
    resid = inputs + jnp.dot(attended, out_weight, preferred_element_type=jnp.float32)
    normed_two, scaled_two, inverse_two = norm_rows(resid, gain_two)
    normed_two_low = normed_two.astype(jnp.bfloat16)
    upper = jnp.dot(normed_two_low, up_weight, preferred_element_type=jnp.float32)
    activated, gelu_back = jax.vjp(jax.nn.gelu, upper)
    activated_low = activated.astype(jnp.bfloat16)
    mixed = (
        resid + jnp.dot(activated_low, down_weight, preferred_element_type=jnp.float32)
    ).astype(jnp.bfloat16)
    grad_result = cotangent.astype(jnp.float32) * local_live[:, None].astype(jnp.float32)
    grad_low = grad_result.astype(jnp.bfloat16)
    down_grad = jnp.einsum("tf,td->fd", activated_low, grad_low, preferred_element_type=jnp.float32)
    grad_active = jnp.einsum("td,fd->tf", grad_low, down_weight, preferred_element_type=jnp.float32)
    grad_upper = gelu_back(grad_active)[0].astype(jnp.bfloat16)
    up_grad = jnp.einsum(
        "td,tf->df", normed_two_low, grad_upper, preferred_element_type=jnp.float32
    )
    grad_normed_two = jnp.einsum(
        "tf,df->td", grad_upper, up_weight, preferred_element_type=jnp.float32
    )
    grad_norm_second, gain_two_grad = norm_back(grad_normed_two, scaled_two, inverse_two, gain_two)
    grad_resid = grad_result + grad_norm_second
    grad_branch = grad_resid.astype(jnp.bfloat16)
    out_grad = jnp.einsum("te,td->ed", attended, grad_branch, preferred_element_type=jnp.float32)
    grad_attended = jnp.einsum(
        "td,ed->te", grad_branch, out_weight, preferred_element_type=jnp.float32
    ).astype(jnp.bfloat16)
    grad_heads = split_heads(grad_attended)
    delta = jnp.sum(
        grad_heads.astype(jnp.float32) * split_heads(attended).astype(jnp.float32), axis=-1
    ).T
    total_rows = local_rows * lax.axis_size("seq")
    key_piece = lax.all_gather(key_rows, "seq", axis=0, tiled=True)
    value_piece = lax.all_gather(value_rows, "seq", axis=0, tiled=True)
    piece_rows = key_piece.shape[0]
    key_heads = split_heads(key_piece)
    weights_low, dscore = score_grads(
        query_heads,
        grad_heads,
        key_heads,
        split_heads(value_piece),
        row_lse,
        delta,
        piece_live(piece_rows),
    )
    grad_query = (
        jnp.einsum("hqk,khd->qhd", dscore, key_heads, preferred_element_type=jnp.float32) * 0.125
    )
    key_terms = (
        jnp.einsum("hqk,qhd->khd", dscore, query_heads, preferred_element_type=jnp.float32) * 0.125
    )
    value_terms = jnp.einsum(
        "hqk,qhd->khd", weights_low, grad_heads, preferred_element_type=jnp.float32
    )
    key_buffer = key_terms
    value_buffer = value_terms
    grad_query, key_buffer, value_buffer = (grad_query, key_buffer, value_buffer)
    grad_keys, grad_values = (
        lax.psum_scatter(
            key_buffer.reshape(total_rows, model_width).astype(jnp.bfloat16),
            "seq",
            scatter_dimension=0,
            tiled=True,
        ).astype(jnp.float32),
        lax.psum_scatter(
            value_buffer.reshape(total_rows, model_width).astype(jnp.bfloat16),
            "seq",
            scatter_dimension=0,
            tiled=True,
        ).astype(jnp.float32),
    )
    grad_qkv = jnp.concatenate(
        [grad_query.reshape(local_rows, model_width), grad_keys, grad_values], axis=1
    ).astype(jnp.bfloat16)
    qkv_grad = jnp.einsum("td,te->de", normed_low, grad_qkv, preferred_element_type=jnp.float32)
    grad_normed_one = jnp.einsum(
        "te,de->td", grad_qkv, qkv_weight, preferred_element_type=jnp.float32
    )
    grad_norm_first, gain_one_grad = norm_back(grad_normed_one, scaled_one, inverse_one, gain_one)
    input_grad = grad_resid + grad_norm_first
    qkv_share, out_share, up_share, down_share, first_share, second_share = (
        lax.psum_scatter(qkv_grad, ("scene", "seq"), scatter_dimension=0, tiled=True),
        lax.psum_scatter(out_grad, ("scene", "seq"), scatter_dimension=0, tiled=True),
        lax.psum_scatter(up_grad, ("scene", "seq"), scatter_dimension=0, tiled=True),
        lax.psum_scatter(down_grad, ("scene", "seq"), scatter_dimension=0, tiled=True),
        lax.psum_scatter(gain_one_grad, ("scene", "seq"), scatter_dimension=0, tiled=True),
        lax.psum_scatter(gain_two_grad, ("scene", "seq"), scatter_dimension=0, tiled=True),
    )
    return (
        mixed,
        input_grad,
        qkv_share,
        out_share,
        up_share,
        down_share,
        first_share,
        second_share,
    )


def solution(mesh):
    in_specs = (
        P(("scene", "seq"), None),
        P("scene"),
        P(("scene", "seq"), None),
        P(("scene", "seq"), None),
        P(("scene", "seq"), None),
        P(("scene", "seq"), None),
        P(("scene", "seq"), None),
        P(),
        P(),
    )
    out_specs = (
        P(("scene", "seq"), None),
        P(("scene", "seq"), None),
        P(("scene", "seq"), None),
        P(("scene", "seq"), None),
        P(("scene", "seq"), None),
        P(("scene", "seq"), None),
        P(("scene", "seq")),
        P(("scene", "seq")),
    )
    return jax.shard_map(
        on_device, mesh=mesh, in_specs=in_specs, out_specs=out_specs, check_vma=False
    )
```

profile of v0, /device:TPU:0, one launch (start us, length us, event | category | flops | bytes accessed | tf_op | source)
XLA Modules:
  0.0 1135.8 jit_solution(7848209360860348284)
XLA Ops:
  7.2 1.6 convert_element_type.98
  8.9 1.2 convert_reduce_fusion
  10.1 1.3 fusion.36
  11.4 63.0 %all-gather.7.cloned.1.call-done = bf16[768,2304]{1,0:T(8,128)(2,1)} async-done(((bf16[24,2304]{1,0:T(8,128)(2,1)}), bf16[768,2304]{1,0:T(8,128)(2,1)}) %all-gather.7.cloned.1.call-update) | async-done | bytes 3538960 | tf_op jit(solution)/shard_map/all_gather | solution.py:64
  74.4 3.6 convolution_convert_fusion
  78.0 1.0 fusion.66
  79.1 0.7 all-gather.11.cloned.1.call-update
  81.3 0.7 convert_element_type.107
  83.1 65.0 %all-gather.9.cloned.1.call-done = bf16[2560,768]{1,0:T(8,128)(2,1)} async-done(((bf16[320,768]{1,0:T(8,128)(2,1)}), bf16[2560,768]{1,0:T(8,128)(2,1)}) %all-gather.9.cloned.1.call-update) | async-done | bytes 3932176 | tf_op jit(solution)/shard_map/all_gather | solution.py:85
  148.1 6.3 copy.29
  154.4 17.1 %select_reduce_fusion = (f32[12,320]{1,0:T(8,128)S(1)}, f32[12,320,2560]{2,1,0:T(8,128)}) fusion(pred[2560]{0:T(1024)(128)(4,1)S(1)} %fusion.51, bf16[320,12,64]{0,2,1:T(8,128)(2,1)S(1)} %bitcast.50, bf16[2560,12,64]{0,2,1:T(8,128)(2,1)} %bitcast.47), kind=kOutput, calls=%fused_computation.3 | convolution fusion | flops 1287778560 | bytes 43763200 | tf_op jit(solution)/shard_map/qhd,khd->hqk/dot_general | solution.py:89
  171.5 47.9 %all-gather.11.cloned.1.call-done = bf16[2560,768]{1,0:T(8,128)(2,1)} async-done(((bf16[320,768]{1,0:T(8,128)(2,1)}), bf16[2560,768]{1,0:T(8,128)(2,1)}) %all-gather.11.cloned.1.call-update) | async-done | bytes 3932176 | tf_op jit(solution)/shard_map/all_gather | solution.py:86
  219.4 6.2 copy.30
  225.6 18.1 %fusion = f32[12,320]{1,0:T(8,128)S(1)} fusion(f32[12,320,2560]{2,1,0:T(8,128)} %get-tuple-element.20, f32[12,320]{1,0:T(8,128)S(1)} %broadcast_maximum_fusion, pred[2560]{0:T(1024)(128)(4,1)S(1)} %fusion.51), kind=kLoop, calls=%fused_computation.4 | loop fusion | flops 39317760 | bytes 39354880 | tf_op jit(solution)/shard_map/reduce_sum | solution.py:97
  243.8 15.2 %divide_convert_fusion = bf16[320,12,64]{0,2,1:T(8,128)(2,1)S(1)} fusion(bf16[2560,12,64]{0,2,1:T(8,128)(2,1)S(1)} %bitcast.55, f32[12,320,2560]{2,1,0:T(8,128)} %get-tuple-element.20, f32[12,320]{1,0:T(8,128)S(1)} %broadcast_maximum_fusion, pred[2560]{0:T(1024)(128)(4,1)S(1)} %fusion.51, f32[320,12]{0,1:T(8,128)S(1)} %bitcast.62), kind=kOutput, calls=%fused_computation.35 | convolution fusion | flops 1298104320 | bytes 43778560 | tf_op jit(solution)/shard_map/hqk,khd->hqd/dot_general | solution.py:98
  259.0 16.4 %all-gather.13.cloned.1.call-done = bf16[768,768]{1,0:T(8,128)(2,1)} async-done(((bf16[24,768]{1,0:T(8,128)(2,1)}), bf16[768,768]{1,0:T(8,128)(2,1)}) %all-gather.13.cloned.1.call-update) | async-done | bytes 1179664 | tf_op jit(solution)/shard_map/all_gather | solution.py:65
  275.4 1.9 fusion.67
  278.2 63.0 %all-gather.15.cloned.1.call-done = bf16[768,3072]{1,0:T(8,128)(2,1)} async-done(((bf16[24,3072]{1,0:T(8,128)(2,1)}), bf16[768,3072]{1,0:T(8,128)(2,1)}) %all-gather.15.cloned.1.call-update) | async-done | bytes 4718608 | tf_op jit(solution)/shard_map/all_gather | solution.py:66
  341.3 6.0 fusion.65
  347.3 59.8 %all-gather.17.cloned.1.call-done = bf16[3072,768]{1,0:T(8,128)(2,1)} async-done(((bf16[96,768]{1,0:T(8,128)(2,1)}), bf16[3072,768]{1,0:T(8,128)(2,1)}) %all-gather.17.cloned.1.call-update) | async-done | bytes 4718608 | tf_op jit(solution)/shard_map/all_gather | solution.py:67
  407.1 7.8 fusion.18
  415.0 2.5 multiply_reduce_fusion.1
  418.5 1.1 copy.31
  419.5 18.2 %fusion.9 = bf16[12,64,2560]{2,1,0:T(8,128)(2,1)} fusion(bf16[320,12,64]{0,2,1:T(8,128)(2,1)} %bitcast.59, f32[12,320,2560]{2,1,0:T(8,128)} %get-tuple-element.20, f32[12,320]{1,0:T(8,128)} %log_add_fusion, pred[2560]{0:T(1024)(128)(4,1)S(1)} %fusion.51), kind=kOutput, calls=%fused_computation.14 | convolution fusion | flops 1299578880 | bytes 43763200 | tf_op jit(solution)/shard_map/hqk,qhd->khd/dot_general | solution.py:162
  437.7 6.3 copy.34
  444.1 1.4 multiply_reduce_fusion
  445.6 26.5 %multiply_convert_fusion = bf16[12,320,2560]{2,1,0:T(8,128)(2,1)} fusion(f32[12,320,2560]{2,1,0:T(8,128)} %get-tuple-element.20, bf16[320,12,64]{0,2,1:T(8,128)(2,1)} %bitcast.61, bf16[2560,12,64]{0,2,1:T(8,128)(2,1)} %bitcast.54, f32[12,320]{1,0:T(8,128)S(1)} %bitcast.63, f32[12,320]{1,0:T(8,128)S(1)} %copy-done.19, pred[2560]{0:T(1024)(128)(4,1)S(1)} %fusion.51), kind=kOutput, calls=%fused_computation | convolution fusion | flops 1317273600 | bytes 63439360 | tf_op jit(solution)/shard_map/qhd,khd->hqk/dot_general | solution.py:37
  472.1 12.6 %multiply_convert_fusion.1 = bf16[12,64,2560]{2,1,0:T(8,128)(2,1)} fusion(bf16[320,12,64]{0,2,1:T(8,128)(2,1)S(1)} %bitcast.51, bf16[12,320,2560]{2,1,0:T(8,128)(2,1)} %multiply_convert_fusion), kind=kOutput, calls=%fused_computation.11 | convolution fusion | flops 1262223360 | bytes 24084480 | tf_op jit(solution)/shard_map/hqk,qhd->khd/dot_general | solution.py:160
  484.7 6.3 copy.32
  491.1 1.0 copy-done.2
  492.1 2.2 fusion.42
  494.3 6.8 fusion.64
  501.2 1.0 copy-done.9
  502.2 8.7 fusion.45
  511.0 10.9 fusion.23
  522.0 5.4 reduce-scatter.21.cloned.1.call-done
  527.4 2.1 copy.35
  529.5 86.1 %reduce-scatter.19.cloned.1.call-done = bf16[320,768]{1,0:T(8,128)(2,1)} async-done(((bf16[2560,768]{1,0:T(8,128)(2,1)}), bf16[320,768]{1,0:T(8,128)(2,1)}) %reduce-scatter.19.cloned.1.call-update) | async-done | bytes 491536
  615.6 2.1 copy.33
  617.7 6.4 fusion.38
  624.1 6.9 fusion.22
  631.0 1.9 fusion.35
  632.9 40.4 %all-reduce.2 = (f32[768]{0:T(1024)S(1)}, f32[768]{0:T(1024)S(1)}) all-reduce(f32[768]{0:T(1024)S(1)} %get-tuple-element.10, f32[768]{0:T(1024)S(1)} %copy-done.23), channel_id=8, replica_groups=mesh['scene'=4,'seq'=8] {'scene','seq'}, use_global_device_ids=true, to_apply=%region_18.19.clone | all-reduce | flops 1536 | bytes 12288
  674.5 1.3 fusion.34
  675.8 44.5 %reduce-scatter.13.cloned.1.call-done = f32[24,768]{1,0:T(8,128)} async-done(((f32[768,768]{1,0:T(8,128)}), f32[24,768]{1,0:T(8,128)}) %reduce-scatter.13.cloned.1.call-update) | async-done | bytes 73744 | tf_op jit(solution)/shard_map/reduce_scatter | solution.py:193
  720.3 142.0 %reduce-scatter.15.cloned.1.call-done = f32[24,3072]{1,0:T(8,128)} async-done(((f32[768,3072]{1,0:T(8,128)}), f32[24,3072]{1,0:T(8,128)}) %reduce-scatter.15.cloned.1.call-update) | async-done | bytes 294928 | tf_op jit(solution)/shard_map/reduce_scatter | solution.py:194
  862.3 141.0 %reduce-scatter.17.cloned.1.call-done = f32[96,768]{1,0:T(8,128)} async-done(((f32[3072,768]{1,0:T(8,128)}), f32[96,768]{1,0:T(8,128)}) %reduce-scatter.17.cloned.1.call-update) | async-done | bytes 294928 | tf_op jit(solution)/shard_map/reduce_scatter | solution.py:195
  1003.3 125.4 %reduce-scatter.11.cloned.1.call-done = f32[24,2304]{1,0:T(8,128)} async-done(((f32[768,2304]{1,0:T(8,128)}), f32[24,2304]{1,0:T(8,128)}) %reduce-scatter.11.cloned.1.call-update) | async-done | bytes 221200 | tf_op jit(solution)/shard_map/reduce_scatter | solution.py:192
  (92 shorter events, 5.5 us)
Async XLA Ops:
  7.2 67.2 %all-gather.7.cloned.1.call-start = ((), (), s32[]{:S(2)}) async-start(), calls=%async_computation.6 | async-start | bytes 3649536 | tf_op jit(solution)/shard_map/all_gather | solution.py:64
  8.8 139.3 %all-gather.9.cloned.1.call-start = ((), (), s32[]{:S(2)}) async-start(), calls=%async_computation.7 | async-start | bytes 4423680 | tf_op jit(solution)/shard_map/all_gather | solution.py:85
  10.1 64.3 %copy-start.15 = (f32[320]{0:T(512)}, f32[320]{0:T(512)S(1)}, u32[]{:S(2)}) copy-start(f32[320]{0:T(512)S(1)} %broadcast_multiply_fusion.5) | copy-start | bytes 3844
  11.4 63.0 %copy-start.17 = (f32[320]{0:T(512)}, f32[320]{0:T(512)S(1)}, u32[]{:S(2)}) copy-start(f32[320]{0:T(512)S(1)} %add_rsqrt_fusion.1) | copy-start | bytes 3844
  78.0 1.9 copy-start.14
  78.0 2.6 copy-start.10
  78.0 3.3 copy-start.11
  79.1 140.3 %all-gather.11.cloned.1.call-start = ((), (), s32[]{:S(2)}) async-start(), calls=%async_computation.8 | async-start | bytes 4423680 | tf_op jit(solution)/shard_map/all_gather | solution.py:86
  79.8 195.6 %all-gather.13.cloned.1.call-start = ((), (), s32[]{:S(2)}) async-start(), calls=%async_computation.9 | async-start | bytes 1216512 | tf_op jit(solution)/shard_map/all_gather | solution.py:65
  80.5 260.8 %all-gather.15.cloned.1.call-start = ((), (), s32[]{:S(2)}) async-start(), calls=%async_computation.10 | async-start | bytes 4866048 | tf_op jit(solution)/shard_map/all_gather | solution.py:66
  81.3 325.8 %all-gather.17.cloned.1.call-start = ((), (), s32[]{:S(2)}) async-start(), calls=%async_computation.11 | async-start | bytes 4866048 | tf_op jit(solution)/shard_map/all_gather | solution.py:67
  82.0 445.4 %reduce-scatter.21.cloned.1.call-start = ((), (), s32[]{:S(2)}) async-start(), calls=%async_computation.17 | async-start | bytes 4423680
  82.8 324.4 %copy-start.20 = (f32[320]{0:T(512)}, f32[320]{0:T(512)S(1)}, u32[]{:S(2)}) copy-start(f32[320]{0:T(512)S(1)} %fusion.55) | copy-start | bytes 3844
  225.6 18.1 %copy-start.4 = (bf16[2560,768]{0,1:T(8,128)(2,1)S(1)}, bf16[2560,768]{0,1:T(8,128)(2,1)}, u32[]{:S(2)}) copy-start(bf16[2560,768]{0,1:T(8,128)(2,1)} %copy.30) | copy-start | bytes 11796484
  243.7 31.6 %copy-start = (bf16[320,768]{1,0:T(8,128)(2,1)S(1)}, bf16[320,768]{1,0:T(8,128)(2,1)}, u32[]{:S(2)}) copy-start(bf16[320,768]{1,0:T(8,128)(2,1)} %param.9) | copy-start | bytes 1474564
  259.0 88.3 %copy-start.1 = (bf16[320,12,64]{0,2,1:T(8,128)(2,1)}, bf16[320,12,64]{0,2,1:T(8,128)(2,1)S(1)}, u32[]{:S(2)}) copy-start(bf16[320,12,64]{0,2,1:T(8,128)(2,1)S(1)} %divide_convert_fusion) | copy-start | bytes 1474564
  259.0 82.3 %copy-start.12 = (f32[768]{0:T(1024)S(1)}, f32[768]{0:T(1024)}, u32[]{:S(2)}) copy-start(f32[768]{0:T(1024)} %param.17) | copy-start | bytes 9220
  278.2 128.9 %copy-start.8 = (bf16[320,768]{1,0:T(8,128)(2,1)S(1)}, bf16[320,768]{1,0:T(8,128)(2,1)}, u32[]{:S(2)}) copy-start(bf16[320,768]{1,0:T(8,128)(2,1)} %param.11) | copy-start | bytes 1474564
  407.1 7.8 copy-start.24
  415.0 2.5 copy-start.7
  415.0 2.5 copy-start.21
  415.0 2.9 copy-start.3
  444.1 1.5 copy-start.19
  444.1 171.5 %reduce-scatter.19.cloned.1.call-start = ((), (), s32[]{:S(2)}) async-start(), calls=%async_computation.16 | async-start | bytes 4423680
  491.0 1.1 copy-start.2
  491.0 229.3 %reduce-scatter.13.cloned.1.call-start = ((), (), s32[]{:S(2)}) async-start(), calls=%async_computation.13 | async-start | bytes 2433024 | tf_op jit(solution)/shard_map/reduce_scatter | solution.py:193
  494.3 368.1 %reduce-scatter.15.cloned.1.call-start = ((), (), s32[]{:S(2)}) async-start(), calls=%async_computation.14 | async-start | bytes 9732096 | tf_op jit(solution)/shard_map/reduce_scatter | solution.py:194
  501.2 1.0 copy-start.9
  501.2 1.0 copy-start.22
  501.2 502.1 %reduce-scatter.17.cloned.1.call-start = ((), (), s32[]{:S(2)}) async-start(), calls=%async_computation.15 | async-start | bytes 9732096 | tf_op jit(solution)/shard_map/reduce_scatter | solution.py:195
  511.0 106.7 %copy-start.13 = (f32[768]{0:T(1024)S(1)}, f32[768]{0:T(1024)}, u32[]{:S(2)}) copy-start(f32[768]{0:T(1024)} %param.16) | copy-start | bytes 9220
  511.0 106.7 %copy-start.16 = (f32[320]{0:T(512)S(1)}, f32[320]{0:T(512)}, u32[]{:S(2)}) copy-start(f32[320]{0:T(512)} %copy-done.15) | copy-start | bytes 3844
  511.0 106.7 %copy-start.18 = (f32[320]{0:T(512)S(1)}, f32[320]{0:T(512)}, u32[]{:S(2)}) copy-start(f32[320]{0:T(512)} %copy-done.17) | copy-start | bytes 3844
  511.0 617.7 %reduce-scatter.11.cloned.1.call-start = ((), (), s32[]{:S(2)}) async-start(), calls=%async_computation.12 | async-start | bytes 7299072 | tf_op jit(solution)/shard_map/reduce_scatter | solution.py:192
  624.1 6.9 copy-start.5
  624.1 6.9 copy-start.6
  624.1 6.9 copy-start.25
  631.0 1.9 copy-start.23
Sparse Core Ops, SparseCore 0:
  11.5 62.8 all-gather.6
  79.2 68.8 all-gather.8
  150.9 68.4 all-gather.10
  222.7 52.6 all-gather.12
  278.7 62.5 all-gather.14
  344.6 62.4 all-gather.16
  444.2 83.1 reduce-scatter.20
  531.5 83.9 reduce-scatter.18
  621.4 98.8 reduce-scatter.12
  727.6 134.6 reduce-scatter.14
  868.8 134.4 reduce-scatter.16
  1010.4 118.2 reduce-scatter.10
where the time goes:
time: 1150 us; the launch traced here: 1140 us
  waiting for transfers between devices  860 us (75%)
  matrix products  156 us (14%)
  blocking collectives  40.4 us (4%)
  local copies, waits for them, and re-layouts  35 us (3%)
  other arithmetic  28.3 us (2%)
  between operations  15.4 us (1%)
    reduce_scatter x1, waiting for transfers between devices, on_device(): lax.psum_scatter(up_grad, ('scene', 'seq'), scatter_dimension=0, tiled=True)  142 us
    reduce_scatter x1, waiting for transfers between devices, on_device(): lax.psum_scatter(down_grad, ('scene', 'seq'), scatter_dimension=0, tiled=...  141 us
    reduce_scatter x1, waiting for transfers between devices, on_device(): lax.psum_scatter(qkv_grad, ('scene', 'seq'), scatter_dimension=0, tiled=T...  125 us
    unnamed x14, waiting for transfers between devices  92.4 us
    all_gather x1, waiting for transfers between devices, on_device(): key_piece = lax.all_gather(key_rows, 'seq', axis=0, tiled=True)  65 us
    all_gather x1, waiting for transfers between devices, on_device(): lax.all_gather(up_part, ('scene', 'seq'), axis=0, tiled=True)  63 us
    all_gather x1, waiting for transfers between devices, on_device(): lax.all_gather(qkv_part, ('scene', 'seq'), axis=0, tiled=True)  63 us
    all_gather x1, waiting for transfers between devices, on_device(): lax.all_gather(down_part, ('scene', 'seq'), axis=0, tiled=True)  59.8 us
  transfers between devices with their start and end apart: 12, of which 12 were waited for; matrix products, arithmetic and copies ran while one was open for 15% of the time, Pallas kernels for 0%

commit v1 on v0

--- a/solution.py
+++ b/solution.py
@@ -6,6 +6,12 @@
 HEADS = 12
 HEAD = 64
 NEG_BIG = -1e30
+
+
+def laid_out(tiles, dim):
+    tiles = jnp.moveaxis(tiles, 0, dim)
+    shape = tiles.shape
+    return tiles.reshape(*shape[:dim], shape[dim] * shape[dim + 1], *shape[dim + 2 :])
 
 
 def norm_rows(values, gain_vector):
@@ -83,7 +89,19 @@
 
     row_max = jnp.full((HEADS, local_rows), NEG_BIG, jnp.float32)
     key_piece = lax.all_gather(key_rows, "seq", axis=0, tiled=True)
-    value_piece = lax.all_gather(value_rows, "seq", axis=0, tiled=True)
+    count = lax.axis_size("seq")
+    pairs = [(i, (i + 1) % count) for i in range(count)]
+    back = [(b, a) for a, b in pairs]
+    lower, upper_2 = ([], [])
+    for turn in range(count - 1):
+        if turn % 2 == 0:
+            lower.append(lax.ppermute(lower[-1] if lower else value_rows, "seq", pairs))
+        else:
+            upper_2.append(lax.ppermute(upper_2[-1] if upper_2 else value_rows, "seq", back))
+    parts = jnp.stack([*lower[::-1], value_rows, *upper_2])
+    shift = lax.axis_index("seq") - len(lower)
+    parts = parts[(jnp.arange(count) - shift) % count]
+    value_piece = laid_out(parts, 0)
     piece_rows = key_piece.shape[0]
     scores = (
         jnp.einsum(

time: 1150 us -> 1160 us (level)
  waiting for transfers between devices: 860 us -> 815 us
  starting transfers between devices: 0.5 us -> 33 us
  local copies, waits for them, and re-layouts: 35 us -> 66.3 us
    ppermute x0 -> x7, waiting for transfers between devices: none -> 75.5 us  [the longest x4 75.5 us: on_device(): lower.append(lax.ppermute(lower[-1] if lower else value_rows, 'seq', pairs))]
    all_gather x1, waiting for transfers between devices: 65 us -> 0.01 us  [on_device(): key_piece = lax.all_gather(key_rows, 'seq', axis=0, tiled=True)]
    ppermute x0 -> x7, starting transfers between devices: none -> 32.3 us  [the longest x3 25.1 us: on_device(): lax.ppermute(upper_2[-1] if upper_2 else value_rows, 'seq', back)]
    all_gather x1, waiting for transfers between devices: 63 us -> 42.5 us  [on_device(): lax.all_gather(up_part, ('scene', 'seq'), axis=0, tiled=True)]
    all_gather x1, waiting for transfers between devices: 16.4 us -> 0.02 us  [on_device(): lax.all_gather(out_part, ('scene', 'seq'), axis=0, tiled=True)]
    all_gather x1, waiting for transfers between devices: 47.9 us -> 32.9 us  [on_device(): value_piece = lax.all_gather(value_rows, 'seq', axis=0, tiled=True)]
    gather x0 -> x2, local copies, waits for them, and re-layouts: none -> 11.9 us  [on_device(): parts = parts[(jnp.arange(count) - shift) % count]]
    unnamed x58 -> x71, local copies, waits for them, and re-layouts: 20 us -> 30.8 us
  transfers between devices with their start and end apart: 12 -> 19, of which waited for: 12 -> 14; matrix products, arithmetic and copies ran while one was open for 15% -> 21% of each run, Pallas kernels for 0% -> 0%
where the time goes in v1:
time: 1160 us
  waiting for transfers between devices  815 us (70%)
  matrix products  156 us (13%)
  local copies, waits for them, and re-layouts  66.3 us (6%)
  blocking collectives  40.5 us (3%)
  starting transfers between devices  33 us (3%)
  other arithmetic  29.1 us (3%)
  between operations  15.5 us (1%)
    reduce_scatter x1, waiting for transfers between devices, on_device(): lax.psum_scatter(up_grad, ('scene', 'seq'), scatter_dimension=0, tiled=True)  142 us
    reduce_scatter x1, waiting for transfers between devices, on_device(): lax.psum_scatter(down_grad, ('scene', 'seq'), scatter_dimension=0, tiled=...  141 us
    reduce_scatter x1, waiting for transfers between devices, on_device(): lax.psum_scatter(qkv_grad, ('scene', 'seq'), scatter_dimension=0, tiled=T...  125 us
    unnamed x14, waiting for transfers between devices  88.7 us
    ppermute x4, waiting for transfers between devices, on_device(): lower.append(lax.ppermute(lower[-1] if lower else value_rows, 'seq', pairs))  75.5 us
    all_gather x1, waiting for transfers between devices, on_device(): lax.all_gather(qkv_part, ('scene', 'seq'), axis=0, tiled=True)  62.9 us
    all_gather x1, waiting for transfers between devices, on_device(): lax.all_gather(down_part, ('scene', 'seq'), axis=0, tiled=True)  59.8 us
    reduce_scatter x1, waiting for transfers between devices, on_device(): lax.psum_scatter(out_grad, ('scene', 'seq'), scatter_dimension=0, tiled=T...  44.5 us
  transfers between devices with their start and end apart: 19, of which 14 were waited for; matrix products, arithmetic and copies ran while one was open for 21% of the time, Pallas kernels for 0%

profile of v1, /device:TPU:0, one launch (start us, length us, event | category | flops | bytes accessed | tf_op | source)
XLA Modules:
  0.0 1155.7 jit_solution(16727150759837373921)
XLA Ops:
  11.4 62.9 %all-gather.7.cloned.1.call-done = bf16[768,2304]{1,0:T(8,128)(2,1)} async-done(((bf16[24,2304]{1,0:T(8,128)(2,1)}), bf16[768,2304]{1,0:T(8,128)(2,1)}) %all-gather.7.cloned.1.call-update) | async-done | bytes 3538960 | tf_op jit(solution)/shard_map/all_gather | solution.py:70
  74.4 3.6 convolution_convert_fusion
  82.8 21.0 %collective-permute-done = bf16[320,768]{1,0:T(8,128)(2,1)S(1)} collective-permute-done((bf16[320,768]{1,0:T(8,128)(2,1)S(1)}, bf16[320,768]{1,0:T(8,128)(2,1)S(1)}, u32[]{:S(2)}, u32[]{:S(2)}) %collective-permute-start) | collective-permute-done | bytes 491552 | tf_op jit(solution)/shard_map/ppermute | solution.py:98
  103.8 4.7 collective-permute-start.4
  108.5 20.0 %collective-permute-done.1 = bf16[320,768]{1,0:T(8,128)(2,1)S(1)} collective-permute-done((bf16[320,768]{1,0:T(8,128)(2,1)S(1)}, bf16[320,768]{1,0:T(8,128)(2,1)S(1)}, u32[]{:S(2)}, u32[]{:S(2)}) %collective-permute-start.1) | collective-permute-done | bytes 491552 | tf_op jit(solution)/shard_map/ppermute | solution.py:98
  128.5 3.0 collective-permute-start.2
  131.5 11.9 %collective-permute-start.5 = (bf16[320,768]{1,0:T(8,128)(2,1)}, bf16[320,768]{1,0:T(8,128)(2,1)}, u32[]{:S(2)}, u32[]{:S(2)}) collective-permute-start(bf16[320,768]{1,0:T(8,128)(2,1)} %collective-permute-done.4), channel_id=1, source_target_pairs={{1,0},{2,1},{3,2},{4,3},{5,4},{6,5},{7,6},{0,7},{9,8},{10,9},{11,1... | collective-permute-start | bytes 1474568 | tf_op jit(solution)/shard_map/ppermute | solution.py:100
  143.5 23.8 %collective-permute-done.2 = bf16[320,768]{1,0:T(8,128)(2,1)} collective-permute-done((bf16[320,768]{1,0:T(8,128)(2,1)S(1)}, bf16[320,768]{1,0:T(8,128)(2,1)}, u32[]{:S(2)}, u32[]{:S(2)}) %collective-permute-start.2) | collective-permute-done | bytes 491552 | tf_op jit(solution)/shard_map/ppermute | solution.py:98
  167.2 2.6 collective-permute-start.3
  171.5 8.5 collective-permute-start.6
  180.0 10.7 collective-permute-done.3
  199.7 1.9 bitcast_dynamic-update-slice_fusion.1
  202.4 4.8 gather_fusion
  207.2 7.1 copy.31
  214.3 8.0 reshape_reshape.3
  222.3 6.3 copy.30
  228.6 17.1 %select_reduce_fusion = (f32[12,320]{1,0:T(8,128)S(1)}, f32[12,320,2560]{2,1,0:T(8,128)}) fusion(pred[2560]{0:T(1024)(128)(4,1)S(1)} %fusion.51, bf16[320,12,64]{0,2,1:T(8,128)(2,1)S(1)} %bitcast.70, bf16[2560,12,64]{0,2,1:T(8,128)(2,1)} %bitcast.67), kind=kOutput, calls=%fused_computation.4 | convolution fusion | flops 1287778560 | bytes 43763200 | tf_op jit(solution)/shard_map/qhd,khd->hqk/dot_general | solution.py:107
  245.7 18.1 %fusion = f32[12,320]{1,0:T(8,128)S(1)} fusion(f32[12,320,2560]{2,1,0:T(8,128)} %get-tuple-element.20, f32[12,320]{1,0:T(8,128)S(1)} %broadcast_maximum_fusion, pred[2560]{0:T(1024)(128)(4,1)S(1)} %fusion.51), kind=kLoop, calls=%fused_computation.5 | loop fusion | flops 39317760 | bytes 39354880 | tf_op jit(solution)/shard_map/reduce_sum | solution.py:115
  263.9 15.3 %divide_convert_fusion = bf16[320,12,64]{0,2,1:T(8,128)(2,1)S(1)} fusion(bf16[2560,12,64]{0,2,1:T(8,128)(2,1)S(1)} %copy-done.4, f32[12,320,2560]{2,1,0:T(8,128)} %get-tuple-element.20, f32[12,320]{1,0:T(8,128)S(1)} %broadcast_maximum_fusion, pred[2560]{0:T(1024)(128)(4,1)S(1)} %fusion.51, f32[320,12]{0,1:T(8,128)S(1)} %bitcast.81), kind=kOutput, calls=%fused_computation.36 | convolution fusion | flops 1298104320 | bytes 43778560 | tf_op jit(solution)/shard_map/hqk,khd->hqd/dot_general | solution.py:116
  279.3 2.1 fusion.69
  281.7 42.5 %all-gather.13.cloned.1.call-done = bf16[768,3072]{1,0:T(8,128)(2,1)} async-done(((bf16[24,3072]{1,0:T(8,128)(2,1)}), bf16[768,3072]{1,0:T(8,128)(2,1)}) %all-gather.13.cloned.1.call-update) | async-done | bytes 4718608 | tf_op jit(solution)/shard_map/all_gather | solution.py:72
  324.2 6.0 fusion.67
  330.2 59.8 %all-gather.15.cloned.1.call-done = bf16[3072,768]{1,0:T(8,128)(2,1)} async-done(((bf16[96,768]{1,0:T(8,128)(2,1)}), bf16[3072,768]{1,0:T(8,128)(2,1)}) %all-gather.15.cloned.1.call-update) | async-done | bytes 4718608 | tf_op jit(solution)/shard_map/all_gather | solution.py:73
  390.1 7.9 fusion.18
  398.0 2.5 multiply_reduce_fusion.1
  403.3 18.3 %fusion.9 = bf16[12,64,2560]{2,1,0:T(8,128)(2,1)} fusion(bf16[320,12,64]{0,2,1:T(8,128)(2,1)} %bitcast.78, f32[12,320,2560]{2,1,0:T(8,128)} %get-tuple-element.20, f32[12,320]{1,0:T(8,128)S(1)} %log_add_fusion, pred[2560]{0:T(1024)(128)(4,1)S(1)} %fusion.51), kind=kOutput, calls=%fused_computation.15 | convolution fusion | flops 1299578880 | bytes 43763200 | tf_op jit(solution)/shard_map/hqk,qhd->khd/dot_general | solution.py:180
  421.7 6.4 copy.36
  428.1 32.9 %all-gather.17.cloned.1.call-done = bf16[2560,768]{1,0:T(8,128)(2,1)} async-done(((bf16[320,768]{1,0:T(8,128)(2,1)}), bf16[2560,768]{1,0:T(8,128)(2,1)}) %all-gather.17.cloned.1.call-update) | async-done | bytes 3932176 | tf_op jit(solution)/shard_map/all_gather | solution.py:162
  461.1 6.3 copy.33
  468.8 26.5 %multiply_convert_fusion = bf16[12,320,2560]{2,1,0:T(8,128)(2,1)} fusion(f32[12,320,2560]{2,1,0:T(8,128)} %get-tuple-element.20, bf16[320,12,64]{0,2,1:T(8,128)(2,1)} %bitcast.80, bf16[2560,12,64]{0,2,1:T(8,128)(2,1)} %bitcast.74, f32[12,320]{1,0:T(8,128)S(1)} %bitcast.82, f32[12,320]{1,0:T(8,128)S(1)} %log_add_fusion, pred[2560]{0:T(1024)(128)(4,1)S(1)} %fusion.51), kind=kOutput, calls=%fused_computation.1 | convolution fusion | flops 1317273600 | bytes 63439360 | tf_op jit(solution)/shard_map/qhd,khd->hqk/dot_general | solution.py:43
  495.3 12.6 %multiply_convert_fusion.1 = bf16[12,64,2560]{2,1,0:T(8,128)(2,1)} fusion(bf16[320,12,64]{0,2,1:T(8,128)(2,1)S(1)} %bitcast.71, bf16[12,320,2560]{2,1,0:T(8,128)(2,1)} %multiply_convert_fusion), kind=kOutput, calls=%fused_computation.12 | convolution fusion | flops 1262223360 | bytes 24084480 | tf_op jit(solution)/shard_map/hqk,qhd->khd/dot_general | solution.py:178
  507.9 6.3 copy.34
  515.3 2.2 fusion.42
  517.6 6.8 fusion.66
  525.4 8.7 fusion.45
  534.3 10.8 fusion.23
  545.1 2.4 reduce-scatter.21.cloned.1.call-done
  547.5 2.1 copy.37
  549.6 86.1 %reduce-scatter.19.cloned.1.call-done = bf16[320,768]{1,0:T(8,128)(2,1)} async-done(((bf16[2560,768]{1,0:T(8,128)(2,1)}), bf16[320,768]{1,0:T(8,128)(2,1)}) %reduce-scatter.19.cloned.1.call-update) | async-done | bytes 491536
  635.6 2.1 copy.35
  637.8 6.4 fusion.38
  644.2 6.9 fusion.22
  651.1 1.9 fusion.35
  653.0 40.5 %all-reduce.2 = (f32[768]{0:T(1024)S(1)}, f32[768]{0:T(1024)S(1)}) all-reduce(f32[768]{0:T(1024)S(1)} %get-tuple-element.10, f32[768]{0:T(1024)S(1)} %copy-done.26), channel_id=8, replica_groups=mesh['scene'=4,'seq'=8] {'scene','seq'}, use_global_device_ids=true, to_apply=%region_18.19.clone | all-reduce | flops 1536 | bytes 12288
  696.0 44.5 %reduce-scatter.13.cloned.1.call-done = f32[24,768]{1,0:T(8,128)} async-done(((f32[768,768]{1,0:T(8,128)}), f32[24,768]{1,0:T(8,128)}) %reduce-scatter.13.cloned.1.call-update) | async-done | bytes 73744 | tf_op jit(solution)/shard_map/reduce_scatter | solution.py:211
  740.5 141.9 %reduce-scatter.15.cloned.1.call-done = f32[24,3072]{1,0:T(8,128)} async-done(((f32[768,3072]{1,0:T(8,128)}), f32[24,3072]{1,0:T(8,128)}) %reduce-scatter.15.cloned.1.call-update) | async-done | bytes 294928 | tf_op jit(solution)/shard_map/reduce_scatter | solution.py:212
  882.4 141.1 %reduce-scatter.17.cloned.1.call-done = f32[96,768]{1,0:T(8,128)} async-done(((f32[3072,768]{1,0:T(8,128)}), f32[96,768]{1,0:T(8,128)}) %reduce-scatter.17.cloned.1.call-update) | async-done | bytes 294928 | tf_op jit(solution)/shard_map/reduce_scatter | solution.py:213
  1023.5 125.1 %reduce-scatter.11.cloned.1.call-done = f32[24,2304]{1,0:T(8,128)} async-done(((f32[768,2304]{1,0:T(8,128)}), f32[24,2304]{1,0:T(8,128)}) %reduce-scatter.11.cloned.1.call-update) | async-done | bytes 221200 | tf_op jit(solution)/shard_map/reduce_scatter | solution.py:210
  (125 shorter events, 29.1 us)
Async XLA Ops:
  7.2 67.2 %all-gather.7.cloned.1.call-start = ((), (), s32[]{:S(2)}) async-start(), calls=%async_computation.6 | async-start | bytes 3649536 | tf_op jit(solution)/shard_map/all_gather | solution.py:70
  8.8 213.4 %all-gather.9.cloned.1.call-start = ((), (), s32[]{:S(2)}) async-start(), calls=%async_computation.7 | async-start | bytes 4423680 | tf_op jit(solution)/shard_map/all_gather | solution.py:91
  10.1 64.3 %copy-start.19 = (f32[320]{0:T(512)}, f32[320]{0:T(512)S(1)}, u32[]{:S(2)}) copy-start(f32[320]{0:T(512)S(1)} %broadcast_multiply_fusion.5) | copy-start | bytes 3844
  11.4 63.0 %copy-start.21 = (f32[320]{0:T(512)}, f32[320]{0:T(512)S(1)}, u32[]{:S(2)}) copy-start(f32[320]{0:T(512)S(1)} %add_rsqrt_fusion.1) | copy-start | bytes 3844
  11.4 67.5 %copy-start.18 = (f32[24,768]{1,0:T(8,128)S(1)}, f32[24,768]{1,0:T(8,128)}, u32[]{:S(2)}) copy-start(f32[24,768]{1,0:T(8,128)} %param.13) | copy-start | bytes 221188
  11.4 68.3 %copy-start.12 = (f32[24,3072]{1,0:T(8,128)S(1)}, f32[24,3072]{1,0:T(8,128)}, u32[]{:S(2)}) copy-start(f32[24,3072]{1,0:T(8,128)} %param.14) | copy-start | bytes 884740
  78.0 2.5 copy-start.13
  78.9 92.6 %copy-start.8 = (bf16[320,768]{1,0:T(8,128)(2,1)}, bf16[320,768]{1,0:T(8,128)(2,1)S(1)}, u32[]{:S(2)}) copy-start(bf16[320,768]{1,0:T(8,128)(2,1)S(1)} %get-tuple-element.17) | copy-start | bytes 1474564
  78.9 200.4 %all-gather.11.cloned.1.call-start = ((), (), s32[]{:S(2)}) async-start(), calls=%async_computation.8 | async-start | bytes 1216512 | tf_op jit(solution)/shard_map/all_gather | solution.py:71
  79.7 244.6 %all-gather.13.cloned.1.call-start = ((), (), s32[]{:S(2)}) async-start(), calls=%async_computation.9 | async-start | bytes 4866048 | tf_op jit(solution)/shard_map/all_gather | solution.py:72
  80.4 309.7 %all-gather.15.cloned.1.call-start = ((), (), s32[]{:S(2)}) async-start(), calls=%async_computation.10 | async-start | bytes 4866048 | tf_op jit(solution)/shard_map/all_gather | solution.py:73
  81.2 379.9 %all-gather.17.cloned.1.call-start = ((), (), s32[]{:S(2)}) async-start(), calls=%async_computation.11 | async-start | bytes 4423680 | tf_op jit(solution)/shard_map/all_gather | solution.py:162
  81.2 22.6 %collective-permute-start = (bf16[320,768]{1,0:T(8,128)(2,1)S(1)}, bf16[320,768]{1,0:T(8,128)(2,1)S(1)}, u32[]{:S(2)}, u32[]{:S(2)}) collective-permute-start(bf16[320,768]{1,0:T(8,128)(2,1)S(1)} %get-tuple-element.17), channel_id=1, source_target_pairs={{0,1},{1,2},{2,3},{3,4},{4,5},{5,6},{6,7},{7,0},{8,9},{9,10},{10,1... | collective-permute-start | bytes 1474568 | tf_op jit(solution)/shard_map/ppermute | solution.py:98
  103.8 24.7 %collective-permute-start.1 = (bf16[320,768]{1,0:T(8,128)(2,1)S(1)}, bf16[320,768]{1,0:T(8,128)(2,1)S(1)}, u32[]{:S(2)}, u32[]{:S(2)}) collective-permute-start(bf16[320,768]{1,0:T(8,128)(2,1)S(1)} %collective-permute-done), channel_id=1, source_target_pairs={{0,1},{1,2},{2,3},{3,4},{4,5},{5,6},{6,7},{7,0},{8,9},{9,10},{10,1... | collective-permute-start | bytes 1474568 | tf_op jit(solution)/shard_map/ppermute | solution.py:98
  103.8 27.8 %collective-permute-start.4 = (bf16[320,768]{1,0:T(8,128)(2,1)S(1)}, bf16[320,768]{1,0:T(8,128)(2,1)}, u32[]{:S(2)}, u32[]{:S(2)}) collective-permute-start(bf16[320,768]{1,0:T(8,128)(2,1)S(1)} %get-tuple-element.17), channel_id=1, source_target_pairs={{1,0},{2,1},{3,2},{4,3},{5,4},{6,5},{7,6},{0,7},{9,8},{10,9},{11,1... | collective-permute-start | bytes 1474568 | tf_op jit(solution)/shard_map/ppermute | solution.py:100
  128.5 42.6 %copy-start.11 = (bf16[320,768]{1,0:T(8,128)(2,1)}, bf16[320,768]{1,0:T(8,128)(2,1)S(1)}, u32[]{:S(2)}) copy-start(bf16[320,768]{1,0:T(8,128)(2,1)S(1)} %collective-permute-done.1) | copy-start | bytes 1474564
  128.5 38.8 %collective-permute-start.2 = (bf16[320,768]{1,0:T(8,128)(2,1)S(1)}, bf16[320,768]{1,0:T(8,128)(2,1)}, u32[]{:S(2)}, u32[]{:S(2)}) collective-permute-start(bf16[320,768]{1,0:T(8,128)(2,1)S(1)} %collective-permute-done.1), channel_id=1, source_target_pairs={{0,1},{1,2},{2,3},{3,4},{4,5},{5,6},{6,7},{7,0},{8,9},{9,10},{10,1... | collective-permute-start | bytes 1474568 | tf_op jit(solution)/shard_map/ppermute | solution.py:98
  131.5 40.0 %collective-permute-start.5 = (bf16[320,768]{1,0:T(8,128)(2,1)}, bf16[320,768]{1,0:T(8,128)(2,1)}, u32[]{:S(2)}, u32[]{:S(2)}) collective-permute-start(bf16[320,768]{1,0:T(8,128)(2,1)} %collective-permute-done.4), channel_id=1, source_target_pairs={{1,0},{2,1},{3,2},{4,3},{5,4},{6,5},{7,6},{0,7},{9,8},{10,9},{11,1... | collective-permute-start | bytes 1474568 | tf_op jit(solution)/shard_map/ppermute | solution.py:100
  167.2 23.5 %collective-permute-start.3 = (bf16[320,768]{1,0:T(8,128)(2,1)}, bf16[320,768]{1,0:T(8,128)(2,1)}, u32[]{:S(2)}, u32[]{:S(2)}) collective-permute-start(bf16[320,768]{1,0:T(8,128)(2,1)} %collective-permute-done.2), channel_id=1, source_target_pairs={{0,1},{1,2},{2,3},{3,4},{4,5},{5,6},{6,7},{7,0},{8,9},{9,10},{10,1... | collective-permute-start | bytes 1474568 | tf_op jit(solution)/shard_map/ppermute | solution.py:98
  171.5 376.0 %reduce-scatter.21.cloned.1.call-start = ((), (), s32[]{:S(2)}) async-start(), calls=%async_computation.17 | async-start | bytes 4423680
  171.5 30.1 %collective-permute-start.6 = (bf16[320,768]{1,0:T(8,128)(2,1)}, bf16[320,768]{1,0:T(8,128)(2,1)S(1)}, u32[]{:S(2)}, u32[]{:S(2)}) collective-permute-start(bf16[320,768]{1,0:T(8,128)(2,1)} %collective-permute-done.5), channel_id=1, source_target_pairs={{1,0},{2,1},{3,2},{4,3},{5,4},{6,5},{7,6},{0,7},{9,8},{10,9},{11,1... | collective-permute-start | bytes 1474568 | tf_op jit(solution)/shard_map/ppermute | solution.py:100
  245.7 18.2 %copy-start.14 = (f32[12,320]{1,0:T(8,128)}, f32[12,320]{1,0:T(8,128)S(1)}, u32[]{:S(2)}) copy-start(f32[12,320]{1,0:T(8,128)S(1)} %get-tuple-element.19) | copy-start | bytes 46084
  245.7 18.2 %copy-start.4 = (bf16[2560,12,64]{0,2,1:T(8,128)(2,1)S(1)}, bf16[2560,12,64]{0,2,1:T(8,128)(2,1)}, u32[]{:S(2)}) copy-start(bf16[2560,12,64]{0,2,1:T(8,128)(2,1)} %reshape_reshape.3) | copy-start | bytes 11796484
  263.9 15.4 %copy-start.17 = (f32[12,320]{1,0:T(8,128)}, f32[12,320]{1,0:T(8,128)S(1)}, u32[]{:S(2)}) copy-start(f32[12,320]{1,0:T(8,128)S(1)} %fusion) | copy-start | bytes 46084
  263.9 15.4 %copy-start = (bf16[320,768]{1,0:T(8,128)(2,1)S(1)}, bf16[320,768]{1,0:T(8,128)(2,1)}, u32[]{:S(2)}) copy-start(bf16[320,768]{1,0:T(8,128)(2,1)} %param.9) | copy-start | bytes 1474564
  279.2 51.0 %copy-start.1 = (bf16[320,12,64]{0,2,1:T(8,128)(2,1)}, bf16[320,12,64]{0,2,1:T(8,128)(2,1)S(1)}, u32[]{:S(2)}) copy-start(bf16[320,12,64]{0,2,1:T(8,128)(2,1)S(1)} %divide_convert_fusion) | copy-start | bytes 1474564
  279.2 45.0 %copy-start.15 = (f32[768]{0:T(1024)S(1)}, f32[768]{0:T(1024)}, u32[]{:S(2)}) copy-start(f32[768]{0:T(1024)} %param.17) | copy-start | bytes 9220
  281.7 108.4 %copy-start.9 = (bf16[320,768]{1,0:T(8,128)(2,1)S(1)}, bf16[320,768]{1,0:T(8,128)(2,1)}, u32[]{:S(2)}) copy-start(bf16[320,768]{1,0:T(8,128)(2,1)} %param.11) | copy-start | bytes 1474564
  281.7 108.4 %copy-start.23 = (f32[320]{0:T(512)S(1)}, f32[320]{0:T(512)}, u32[]{:S(2)}) copy-start(f32[320]{0:T(512)} %fusion.55) | copy-start | bytes 3844
  390.1 7.9 copy-start.27
  398.0 2.5 copy-start.7
  398.0 2.5 copy-start.24
  398.0 2.9 copy-start.3
  428.1 207.6 %reduce-scatter.19.cloned.1.call-start = ((), (), s32[]{:S(2)}) async-start(), calls=%async_computation.16 | async-start | bytes 4423680
  514.2 1.1 copy-start.2
  514.3 226.2 %reduce-scatter.13.cloned.1.call-start = ((), (), s32[]{:S(2)}) async-start(), calls=%async_computation.13 | async-start | bytes 2433024 | tf_op jit(solution)/shard_map/reduce_scatter | solution.py:211
  517.5 364.9 %reduce-scatter.15.cloned.1.call-start = ((), (), s32[]{:S(2)}) async-start(), calls=%async_computation.14 | async-start | bytes 9732096 | tf_op jit(solution)/shard_map/reduce_scatter | solution.py:212
  524.4 1.0 copy-start.10
  524.4 1.0 copy-start.25
  524.4 499.1 %reduce-scatter.17.cloned.1.call-start = ((), (), s32[]{:S(2)}) async-start(), calls=%async_computation.15 | async-start | bytes 9732096 | tf_op jit(solution)/shard_map/reduce_scatter | solution.py:213
  534.2 103.6 %copy-start.16 = (f32[768]{0:T(1024)S(1)}, f32[768]{0:T(1024)}, u32[]{:S(2)}) copy-start(f32[768]{0:T(1024)} %param.16) | copy-start | bytes 9220
  534.2 103.6 %copy-start.20 = (f32[320]{0:T(512)S(1)}, f32[320]{0:T(512)}, u32[]{:S(2)}) copy-start(f32[320]{0:T(512)} %copy-done.19) | copy-start | bytes 3844
  534.2 103.6 %copy-start.22 = (f32[320]{0:T(512)S(1)}, f32[320]{0:T(512)}, u32[]{:S(2)}) copy-start(f32[320]{0:T(512)} %copy-done.21) | copy-start | bytes 3844
  534.2 614.4 %reduce-scatter.11.cloned.1.call-start = ((), (), s32[]{:S(2)}) async-start(), calls=%async_computation.12 | async-start | bytes 7299072 | tf_op jit(solution)/shard_map/reduce_scatter | solution.py:210
  644.2 6.9 copy-start.5
  644.2 6.9 copy-start.6
  644.2 6.9 copy-start.28
  651.1 1.9 copy-start.26
Sparse Core Ops, SparseCore 0:
  11.5 62.8 all-gather.6
  79.0 121.0 all-gather.8
  203.6 54.6 all-gather.10
  261.7 62.5 all-gather.12
  327.6 62.4 all-gather.14
  392.1 68.8 all-gather.16
  464.7 82.7 reduce-scatter.20
  551.6 83.9 reduce-scatter.18
  641.5 98.9 reduce-scatter.12
  747.8 134.5 reduce-scatter.14
  888.9 134.6 reduce-scatter.16
  1030.6 118.0 reduce-scatter.10
